TPU v7x, 32 devices: a whole 2x2x4 slice. The times are simulated.
32 devices in a mesh: dp: 16 (over z, y, x), mp: 2 (over core).
Axes of the slice: x: 2, y: 2, z: 4, core: 2. Of those that a mesh axis runs over, the one named last changes fastest.
Arguments:
- tokens: bfloat16 [32768, 768], P(('dp', 'mp')), may hold values from -6 to 6
- out_grad: bfloat16 [32768, 768], P(('dp', 'mp')), may hold values from -6 to 6
- image_lengths: int32 [16, 69], P('dp'), may hold values from 0 to 98, as said below
- group_of_block: int32 [16], P('dp'), may hold values from 0 to 2, as said below
- norm_gains: float32 [2, 768], replicated, may hold values from 0.5 to 1.5
- row_biases: float32 [4, 768], replicated, may hold values from -1.5 to 1.5
- w_qkv: bfloat16 [3, 768, 768], P(None, None, 'mp'), may hold values from -0.21875 to 0.21875
- qv_bias: float32 [2, 768], P(None, 'mp'), may hold values from -1.5 to 1.5
- w_out: bfloat16 [768, 768], P('mp'), may hold values from -0.875 to 0.875
- w_fc1: bfloat16 [768, 3072], P(None, 'mp'), may hold values from -0.21875 to 0.21875
- b_fc1: float32 [3072], P('mp'), may hold values from -1.5 to 1.5
- w_fc2: bfloat16 [3072, 768], P('mp'), may hold values from -0.109375 to 0.109375
Outputs:
- output: bfloat16 [32768, 768], P(('dp', 'mp'))
- tokens_grad: float32 [32768, 768], P(('dp', 'mp'))
- norm_gains_grad: float32 [2, 768], replicated
- row_biases_grad: float32 [4, 768], replicated
- w_qkv_grad: float32 [3, 768, 768], P(None, None, 'mp')
- qv_bias_grad: float32 [2, 768], P(None, 'mp')
- w_out_grad: float32 [768, 768], P('mp')
- w_fc1_grad: float32 [768, 3072], P(None, 'mp')
- b_fc1_grad: float32 [3072], P('mp')
- w_fc2_grad: float32 [3072, 768], P('mp')
Inputs may be any that keep to these rules, and one draw needn't show every extreme that they name: `image_lengths`: row b lists the patch counts of the images packed in block b from the first slot on; each image has 30 to 98 patches, slots after the last image hold 0, the counts of a row sum to at most 2048 and the rest of the block is padding; every block has an image of 98 patches. `group_of_block`: entry b is the dataset group of block b; it never falls along the blocks, and each of the 3 groups holds at least one block.
All inputs are finite; a program needn't handle non-finite values.
Results may differ from a plain program's by a relative error of at most 0.015.
Values may be sent and summed in bfloat16 or wider, within the bound.
No kernel may reach another device: no remote copies, remote signals or barrier semaphores. Data moves between devices by JAX's collectives and lax.ppermute only.
A program may use at most 256 MiB of HBM per device.

v0:
```python
import jax
import jax.numpy as jnp
from jax import lax
from jax.sharding import PartitionSpec as P

HEAD_DIM = 64
GROUPS = 3
LEN_NORM = 64


def layer_norm(values, gain_vec, shift_vec):
    center = values - jnp.mean(values, axis=-1, keepdims=True)
    spread = jnp.mean(center * center, axis=-1, keepdims=True)
    return center * lax.rsqrt(spread + 1e-06) * gain_vec + shift_vec


def gelu_tanh(values):
    return (
        0.5
        * values
        * (1.0 + jnp.tanh(0.7978845608028654 * (values + 0.044715 * values * values * values)))
    )


def image_rows(lengths, row_count):
    image_ends = jnp.cumsum(lengths)
    position = jnp.arange(row_count, dtype=jnp.int32)
    segment = jnp.sum((position[:, None] >= image_ends[None, :]).astype(jnp.int32), axis=1)
    slot_ids = jnp.arange(lengths.shape[0], dtype=jnp.int32)
    row_length = jnp.sum(
        jnp.where(segment[:, None] == slot_ids[None, :], lengths[None, :], 0), axis=1
    )
    return (segment, row_length)


def score_block(query_block, segment_block, keys_all, segment, score_scale):
    scores = (
        jnp.einsum("qhd,khd->hqk", query_block, keys_all, preferred_element_type=jnp.float32)
        * score_scale
    )
    return jnp.where((segment_block[:, None] == segment[None, :])[None], scores, -1000000000.0)


def local(
    tokens,
    out_grad,
    image_lengths,
    group_of_block,
    norm_gains,
    row_biases,
    w_qkv,
    qv_bias,
    w_out,
    w_fc1,
    b_fc1,
    w_fc2,
):
    own_rows = tokens.shape[0]
    row_count = own_rows * lax.axis_size("mp")
    first_row = lax.axis_index("mp") * own_rows
    segment, row_length = image_rows(image_lengths[0], row_count)
    images = jnp.sum((image_lengths[0] > 0).astype(jnp.float32))
    member = (group_of_block[0] == jnp.arange(GROUPS, dtype=jnp.int32)).astype(jnp.float32)
    group_images = lax.psum(member * images, "dp")
    group_roots = jnp.sqrt(group_images)
    factor = jnp.sum(group_images) / (group_roots * jnp.sum(group_roots))
    block_factor = jnp.sum(member * factor)
    own_length = lax.dynamic_slice_in_dim(row_length, first_row, own_rows)
    weight_row = (
        block_factor
        * LEN_NORM
        * (own_length > 0).astype(jnp.float32)
        / jnp.maximum(own_length, 1).astype(jnp.float32)
    )
    tokens_f = tokens.astype(jnp.float32)
    normed, norm_pull = jax.vjp(layer_norm, tokens_f, norm_gains[0], row_biases[0])
    normed_low = normed.astype(jnp.bfloat16)
    normed_all = lax.all_gather(normed_low, "mp", axis=0, tiled=True)
    projected = jnp.einsum("rd,tde->tre", normed_all, w_qkv, preferred_element_type=jnp.float32)
    bias_three = jnp.stack([qv_bias[0], jnp.zeros_like(qv_bias[0]), qv_bias[1]])
    projected = (projected + bias_three[:, None, :]).astype(jnp.bfloat16)
    local_width = w_qkv.shape[2]
    head_count = local_width // HEAD_DIM
    shaped = projected.reshape(3, row_count, head_count, HEAD_DIM)
    queries, keys_all, values_all = (shaped[0], shaped[1], shaped[2])
    block_rows = min(512, row_count)
    block_count = row_count // block_rows
    score_scale = HEAD_DIM ** (-0.5)
    query_blocks = queries.reshape(block_count, block_rows, head_count, HEAD_DIM)
    segment_blocks = segment.reshape(block_count, block_rows)

    def forward_block(pieces):
        query_block, segment_block = pieces
        scores = score_block(query_block, segment_block, keys_all, segment, score_scale)
        top_score = jnp.max(scores, axis=-1, keepdims=True)
        exponent = jnp.exp(scores - top_score)
        total = jnp.sum(exponent, axis=-1, keepdims=True)
        weights = (exponent / total).astype(jnp.bfloat16)
        context = jnp.einsum(
            "hqk,khd->qhd", weights, values_all, preferred_element_type=jnp.float32
        )
        return (context, (top_score + jnp.log(total))[:, :, 0])

    context, log_total = lax.map(forward_block, (query_blocks, segment_blocks))
    context_low = context.reshape(row_count, local_width).astype(jnp.bfloat16)
    piece = context_low
    attention = lax.psum_scatter(
        jnp.dot(piece, w_out, preferred_element_type=jnp.float32).astype(jnp.bfloat16),
        "mp",
        scatter_dimension=0,
        tiled=True,
    ).astype(jnp.float32)
    hidden_one = tokens_f + attention + row_biases[2]
    normed_two, norm_two_pull = jax.vjp(layer_norm, hidden_one, norm_gains[1], row_biases[1])
    normed_two_all = lax.all_gather(normed_two.astype(jnp.bfloat16), "mp", axis=0, tiled=True)
    before = jnp.dot(normed_two_all, w_fc1, preferred_element_type=jnp.float32) + b_fc1
    activated, gelu_pull = jax.vjp(gelu_tanh, before)
    activated_low = activated.astype(jnp.bfloat16)
    piece = activated_low
    mlp_out = lax.psum_scatter(
        jnp.dot(piece, w_fc2, preferred_element_type=jnp.float32).astype(jnp.bfloat16),
        "mp",
        scatter_dimension=0,
        tiled=True,
    ).astype(jnp.float32)
    output = (hidden_one + mlp_out + row_biases[3]).astype(jnp.bfloat16)
    out_cot = out_grad.astype(jnp.float32) * weight_row[:, None]
    out_cot_all = lax.all_gather(out_cot.astype(jnp.bfloat16), "mp", axis=0, tiled=True)
    grad_fc2 = jnp.einsum(
        "rf,rd->fd", activated_low, out_cot_all, preferred_element_type=jnp.float32
    )
    grad_act = jnp.einsum("rd,fd->rf", out_cot_all, w_fc2, preferred_element_type=jnp.float32)
    grad_before = gelu_pull(grad_act)[0].astype(jnp.bfloat16)
    grad_bfc1 = jnp.sum(grad_before.astype(jnp.float32), axis=0)
    grad_fc1 = jnp.einsum(
        "rd,rf->df", normed_two_all, grad_before, preferred_element_type=jnp.float32
    )
    piece = grad_before
    grad_norm_two = lax.psum_scatter(
        jnp.einsum("rf,df->rd", piece, w_fc1, preferred_element_type=jnp.float32).astype(
            jnp.bfloat16
        ),
        "mp",
        scatter_dimension=0,
        tiled=True,
    ).astype(jnp.float32)
    grad_hidden, grad_gain_two, grad_shift_two = norm_two_pull(grad_norm_two)
    grad_hidden = grad_hidden + out_cot
    grad_hidden_all = lax.all_gather(grad_hidden.astype(jnp.bfloat16), "mp", axis=0, tiled=True)
    grad_out = jnp.einsum(
        "rc,rd->cd", context_low, grad_hidden_all, preferred_element_type=jnp.float32
    )
    grad_context = jnp.einsum(
        "rd,cd->rc", grad_hidden_all, w_out, preferred_element_type=jnp.float32
    ).astype(jnp.bfloat16)
    context_blocks = grad_context.reshape(block_count, block_rows, head_count, HEAD_DIM)

    def backward_block(carry, pieces):
        grad_keys, grad_values = carry
        query_block, segment_block, log_block, grad_block = pieces
        scores = score_block(query_block, segment_block, keys_all, segment, score_scale)
        probs = jnp.exp(scores - log_block[:, :, None])
        grad_values = grad_values + jnp.einsum(
            "hqk,qhd->khd",
            probs.astype(jnp.bfloat16),
            grad_block,
            preferred_element_type=jnp.float32,
        )
        grad_probs = jnp.einsum(
            "qhd,khd->hqk", grad_block, values_all, preferred_element_type=jnp.float32
        )
        grad_scores = probs * (grad_probs - jnp.sum(probs * grad_probs, axis=-1, keepdims=True))
        grad_scores = grad_scores.astype(jnp.bfloat16)
        grad_query = (
            jnp.einsum("hqk,khd->qhd", grad_scores, keys_all, preferred_element_type=jnp.float32)
            * score_scale
        )
        grad_keys = (
            grad_keys
            + jnp.einsum(
                "hqk,qhd->khd", grad_scores, query_block, preferred_element_type=jnp.float32
            )
            * score_scale
        )
        return ((grad_keys, grad_values), grad_query)

    zero_heads = jnp.zeros((row_count, head_count, HEAD_DIM), jnp.float32)
    (grad_keys, grad_values), grad_queries = lax.scan(
        backward_block,
        (zero_heads, zero_heads),
        (query_blocks, segment_blocks, log_total, context_blocks),
    )
    grad_projected = jnp.stack(
        [
            grad_queries.reshape(row_count, local_width),
            grad_keys.reshape(row_count, local_width),
            grad_values.reshape(row_count, local_width),
        ]
    ).astype(jnp.bfloat16)
    grad_qv_bias = jnp.stack(
        [
            jnp.sum(grad_projected[0].astype(jnp.float32), axis=0),
            jnp.sum(grad_projected[2].astype(jnp.float32), axis=0),
        ]
    )
    grad_qkv = jnp.einsum(
        "rd,tre->tde", normed_all, grad_projected, preferred_element_type=jnp.float32
    )
    piece = grad_projected
    grad_norm_one = lax.psum_scatter(
        jnp.einsum("tre,tde->rd", piece, w_qkv, preferred_element_type=jnp.float32).astype(
            jnp.bfloat16
        ),
        "mp",
        scatter_dimension=0,
        tiled=True,
    ).astype(jnp.float32)
    grad_input, grad_gain_one, grad_shift_one = norm_pull(grad_norm_one)
    grad_input = grad_input + grad_hidden
    gain_grads, shift_grads = lax.psum(
        (
            jnp.stack([grad_gain_one, grad_gain_two]),
            jnp.stack(
                [
                    grad_shift_one,
                    grad_shift_two,
                    jnp.sum(grad_hidden, axis=0),
                    jnp.sum(out_cot, axis=0),
                ]
            ),
        ),
        ("dp", "mp"),
    )
    grad_qkv, grad_qv_bias, grad_out, grad_fc1, grad_bfc1, grad_fc2 = lax.psum(
        (grad_qkv, grad_qv_bias, grad_out, grad_fc1, grad_bfc1, grad_fc2), "dp"
    )
    return (
        output,
        grad_input,
        gain_grads,
        shift_grads,
        grad_qkv,
        grad_qv_bias,
        grad_out,
        grad_fc1,
        grad_bfc1,
        grad_fc2,
    )


def solution(mesh):
    placed = (
        P(("dp", "mp"), None),
        P(("dp", "mp"), None),
        P("dp", None),
        P("dp"),
        P(),
        P(),
        P(None, None, "mp"),
        P(None, "mp"),
        P("mp", None),
        P(None, "mp"),
        P("mp"),
        P("mp", None),
    )
    return jax.shard_map(
        local,
        mesh=mesh,
        in_specs=placed,
        out_specs=(
            P(("dp", "mp"), None),
            P(("dp", "mp"), None),
            P(),
            P(),
            P(None, None, "mp"),
            P(None, "mp"),
            P("mp", None),
            P(None, "mp"),
            P("mp"),
            P("mp", None),
        ),
        check_vma=False,
    )
```

profile of v0, /device:TPU:0, one launch (start us, length us, event | category | flops | bytes accessed | tf_op | source)
XLA Modules:
  0.0 1192.0 jit_solution(15143467741998065962)
XLA Ops:
  15.6 14.2 %all-gather.5.cloned.1.call-done = bf16[2048,768]{1,0:T(8,128)(2,1)} async-done(((bf16[1024,768]{1,0:T(8,128)(2,1)}), bf16[2048,768]{1,0:T(8,128)(2,1)}) %all-gather.5.cloned.1.call-update) | async-done | bytes 3145744 | tf_op jit(solution)/shard_map/all_gather | solution.py:78
  29.8 6.3 fusion.45
  38.5 4.0 reshape_squeeze.3
  46.7 159.6 %while.27 = (s32[]{:T(128)}, bf16[4,512,6,64]{1,3,2,0:T(8,128)(2,1)}, f32[4,6,512]{2,1,0:T(8,128)S(1)}, s32[4,512]{1,0:T(4,128)S(1)}, s32[2048]{0:T(1024)S(1)}, ...) while((s32[]{:T(128)}, ...), condition=%wide.region_7.8_spmd, body=%wide.region_4.7_spmd.sunk | while | flops 1687155712 | bytes 103024832 | solution.py:104
  47.3 14.3 %fusion.128 = (f32[6,512]{1,0:T(8,128)S(1)}, f32[6,512,2048]{2,1,0:T(8,128)}) fusion(pred[512,2048]{1,0:T(8,128)(4,1)S(1)} %broadcast_compare_fusion.4, bf16[2048,6,64]{0,2,1:T(8,128)(2,1)} %get-tuple-element.469, bf16[4,512,6,64]{1,3,2,0:T(8,128)(2,1)} %get-tuple-element.468, s32[]{:T(128)S(6)} %copy.67), kind=kOutput, calls=%fused_computation.3.clone.1 | convolution fusion | flops 824177664 | bytes 28192772 | tf_op jit(solution)/shard_map/while/body/eval_jaxpr/qhd,khd->hqk/dot_general | solution.py:38
  61.6 12.1 %fusion.129 = f32[6,512]{1,0:T(8,128)S(1)} fusion(f32[6,512,2048]{2,1,0:T(8,128)} %get-tuple-element.430, f32[6,512]{1,0:T(8,128)S(1)} %get-tuple-element.431, pred[512,2048]{1,0:T(8,128)(4,1)S(1)} %broadcast_compare_fusion.4), kind=kLoop, calls=%fused_computation.4.clone.1 | loop fusion | flops 25162752 | bytes 26238976 | tf_op jit(solution)/shard_map/while/body/eval_jaxpr/reduce_sum | solution.py:97
  73.7 11.6 fusion.130
  87.2 14.3 %fusion.128 = (f32[6,512]{1,0:T(8,128)S(1)}, f32[6,512,2048]{2,1,0:T(8,128)}) fusion(pred[512,2048]{1,0:T(8,128)(4,1)S(1)} %broadcast_compare_fusion.4, bf16[2048,6,64]{0,2,1:T(8,128)(2,1)} %get-tuple-element.469, bf16[4,512,6,64]{1,3,2,0:T(8,128)(2,1)} %get-tuple-element.468, s32[]{:T(128)S(6)} %copy.67), kind=kOutput, calls=%fused_computation.3.clone.1 | convolution fusion | flops 824177664 | bytes 28192772 | tf_op jit(solution)/shard_map/while/body/eval_jaxpr/qhd,khd->hqk/dot_general | solution.py:38
  101.5 12.1 %fusion.129 = f32[6,512]{1,0:T(8,128)S(1)} fusion(f32[6,512,2048]{2,1,0:T(8,128)} %get-tuple-element.430, f32[6,512]{1,0:T(8,128)S(1)} %get-tuple-element.431, pred[512,2048]{1,0:T(8,128)(4,1)S(1)} %broadcast_compare_fusion.4), kind=kLoop, calls=%fused_computation.4.clone.1 | loop fusion | flops 25162752 | bytes 26238976 | tf_op jit(solution)/shard_map/while/body/eval_jaxpr/reduce_sum | solution.py:97
  113.6 11.6 fusion.130
  127.1 14.3 %fusion.128 = (f32[6,512]{1,0:T(8,128)S(1)}, f32[6,512,2048]{2,1,0:T(8,128)}) fusion(pred[512,2048]{1,0:T(8,128)(4,1)S(1)} %broadcast_compare_fusion.4, bf16[2048,6,64]{0,2,1:T(8,128)(2,1)} %get-tuple-element.469, bf16[4,512,6,64]{1,3,2,0:T(8,128)(2,1)} %get-tuple-element.468, s32[]{:T(128)S(6)} %copy.67), kind=kOutput, calls=%fused_computation.3.clone.1 | convolution fusion | flops 824177664 | bytes 28192772 | tf_op jit(solution)/shard_map/while/body/eval_jaxpr/qhd,khd->hqk/dot_general | solution.py:38
  141.3 12.1 %fusion.129 = f32[6,512]{1,0:T(8,128)S(1)} fusion(f32[6,512,2048]{2,1,0:T(8,128)} %get-tuple-element.430, f32[6,512]{1,0:T(8,128)S(1)} %get-tuple-element.431, pred[512,2048]{1,0:T(8,128)(4,1)S(1)} %broadcast_compare_fusion.4), kind=kLoop, calls=%fused_computation.4.clone.1 | loop fusion | flops 25162752 | bytes 26238976 | tf_op jit(solution)/shard_map/while/body/eval_jaxpr/reduce_sum | solution.py:97
  153.5 11.6 fusion.130
  166.9 14.3 %fusion.128 = (f32[6,512]{1,0:T(8,128)S(1)}, f32[6,512,2048]{2,1,0:T(8,128)}) fusion(pred[512,2048]{1,0:T(8,128)(4,1)S(1)} %broadcast_compare_fusion.4, bf16[2048,6,64]{0,2,1:T(8,128)(2,1)} %get-tuple-element.469, bf16[4,512,6,64]{1,3,2,0:T(8,128)(2,1)} %get-tuple-element.468, s32[]{:T(128)S(6)} %copy.67), kind=kOutput, calls=%fused_computation.3.clone.1 | convolution fusion | flops 824177664 | bytes 28192772 | tf_op jit(solution)/shard_map/while/body/eval_jaxpr/qhd,khd->hqk/dot_general | solution.py:38
  181.2 12.1 %fusion.129 = f32[6,512]{1,0:T(8,128)S(1)} fusion(f32[6,512,2048]{2,1,0:T(8,128)} %get-tuple-element.430, f32[6,512]{1,0:T(8,128)S(1)} %get-tuple-element.431, pred[512,2048]{1,0:T(8,128)(4,1)S(1)} %broadcast_compare_fusion.4), kind=kLoop, calls=%fused_computation.4.clone.1 | loop fusion | flops 25162752 | bytes 26238976 | tf_op jit(solution)/shard_map/while/body/eval_jaxpr/reduce_sum | solution.py:97
  193.3 11.6 fusion.130
  210.6 3.5 convolution_convert_fusion
  214.2 12.2 %reduce-scatter.5.cloned.1.call-done = bf16[1024,768]{1,0:T(8,128)(2,1)} async-done(((bf16[2048,768]{1,0:T(8,128)(2,1)}), bf16[1024,768]{1,0:T(8,128)(2,1)}) %reduce-scatter.5.cloned.1.call-update) | async-done | bytes 1572880 | tf_op jit(solution)/shard_map/reduce_scatter | solution.py:107
  234.2 41.9 %psum.63 = f32[3]{0:T(128)S(1)} all-reduce(f32[3]{0:T(128)S(1)} %compare_select_fusion.1), channel_id=1, replica_groups=mesh['dp'=16,'mp'=2] {'dp'}, use_global_device_ids=true, to_apply=%region_14.15 | all-reduce | flops 3 | bytes 24 | tf_op jit(solution)/shard_map/psum | solution.py:64
  282.4 13.7 %multiply_convert_fusion.1 = (bf16[2048,1536]{1,0:T(8,128)(2,1)}, f32[2048,1536]{1,0:T(8,128)}) fusion(f32[1536]{0:T(1024)S(1)} %copy-done.48, bf16[2048,768]{1,0:T(8,128)(2,1)} %all-gather.7.cloned.1.call-done, bf16[768,1536]{1,0:T(8,128)(2,1)S(1)} %copy-done), kind=kOutput, calls=%fused_computation.58 | convolution fusion | flops 4863295488 | bytes 24385536 | tf_op jit(solution)/shard_map/dot_general | solution.py:116
  296.1 19.5 %convert_reduce_fusion = (f32[1536]{0:T(1024)}, bf16[2048,1536]{1,0:T(8,128)(2,1)S(1)}) fusion(bf16[2048,768]{1,0:T(8,128)(2,1)} %all-gather.9.cloned.1.call-done, bf16[1536,768]{1,0:T(8,128)(2,1)} %param.27, f32[2048,1536]{1,0:T(8,128)} %get-tuple-element.318, f32[1536]{0:T(1024)S(1)} %copy-done.48), kind=kOutput, calls=%fused_computation.57 | convolution fusion | flops 4916771328 | bytes 24391680 | tf_op jit(solution)/shard_map/rd,fd->rf/dot_general | solution.py:132
  318.2 6.4 convolution_convert_fusion.1
  326.3 9.7 convolution_convert_fusion.2
  337.4 3.9 convert_reduce_fusion.2
  341.3 4.2 fusion.56
  346.4 5.6 fusion.77
  355.0 13.4 %all-gather.11.cloned.1.call-done = bf16[2048,768]{1,0:T(8,128)(2,1)} async-done(((bf16[1024,768]{1,0:T(8,128)(2,1)}), bf16[2048,768]{1,0:T(8,128)(2,1)}) %all-gather.11.cloned.1.call-update) | async-done | bytes 3145744 | tf_op jit(solution)/shard_map/all_gather | solution.py:149
  368.4 4.9 convolution_convert_fusion.3
  381.7 333.3 %while.28 = (s32[]{:T(128)}, f32[2048,6,64]{0,2,1:T(8,128)}, f32[2048,6,64]{0,2,1:T(8,128)}, bf16[4,512,6,64]{1,3,2,0:T(8,128)(2,1)}, bf16[4,512,6,64]{1,3,2,0:T...) while((s32[]{:T(128)}, f32[2048,6,64]{0,2,1:T(8,128)}, ...), condition=%wide.region_23.24_spmd.clone, body=%wide.region_21.23_spmd.clone.sunk | while | flops 4126077952 | bytes 212699312 | solution.py:188
  382.6 11.0 fusion.140
  393.7 12.8 %bitcast_add_fusion.5 = f32[2048,6,64]{0,2,1:T(8,128)} fusion(f32[2048,6,64]{0,2,1:T(8,128)} %get-tuple-element.487, f32[6,512,2048]{2,1,0:T(8,128)} %fusion.140, f32[6,512]{1,0:T(8,128)S(1)} %dynamic-slice_bitcast_fusion.2, pred[512,2048]{1,0:T(8,128)(4,1)S(1)} %broadcast_compare_fusion.5, pred[]{:T(512)S(6)} %compare.3, ...), kind=kOutput, calls=%fused_computation.23.clone.1 | convolution fusion | flops 832045056 | bytes 32911364 | tf_op jit(solution)/shard_map/while/body/eval_jaxpr/hqk,qhd->khd/dot_general | solution.py:163
  406.5 18.1 %multiply_reduce_fusion.3 = (f32[6,512]{1,0:T(8,128)S(1)}, f32[6,512,2048]{2,1,0:T(8,128)}) fusion(f32[6,512,2048]{2,1,0:T(8,128)} %fusion.140, f32[6,512]{1,0:T(8,128)S(1)} %dynamic-slice_bitcast_fusion.2, pred[512,2048]{1,0:T(8,128)(4,1)S(1)} %broadcast_compare_fusion.5, bf16[2048,6,64]{0,2,1:T(8,128)(2,1)} %get-tuple-element.508, ...), kind=kOutput, calls=%fused_computation.18.clone.1 | convolution fusion | flops 836760576 | bytes 53370884 | tf_op jit(solution)/shard_map/while/body/eval_jaxpr/qhd,khd->hqk/dot_general | solution.py:169
  424.6 21.3 %multiply_convert_fusion.3 = bf16[6,512,2048]{2,1,0:T(8,128)(2,1)} fusion(f32[6,512,2048]{2,1,0:T(8,128)} %get-tuple-element.443, f32[6,512,2048]{2,1,0:T(8,128)} %fusion.140, f32[6,512]{1,0:T(8,128)S(1)} %get-tuple-element.444, f32[6,512]{1,0:T(8,128)S(1)} %dynamic-slice_bitcast_fusion.2, pred[512,2048]{1,0:T(8,128)(4,1)S(1)} %broadcast_compare_fusion.5), kind=kLoop, calls=%fused_computation.17.clone.1 | loop fusion | flops 37748736 | bytes 63987712 | tf_op jit(solution)/shard_map/while/body/eval_jaxpr/convert_element_type | solution.py:173
  445.8 9.3 fusion.141
  455.1 8.7 bitcast_add_fusion.4
  464.5 11.0 fusion.140
  475.5 13.7 %bitcast_add_fusion.5 = f32[2048,6,64]{0,2,1:T(8,128)} fusion(f32[2048,6,64]{0,2,1:T(8,128)} %get-tuple-element.487, f32[6,512,2048]{2,1,0:T(8,128)} %fusion.140, f32[6,512]{1,0:T(8,128)S(1)} %dynamic-slice_bitcast_fusion.2, pred[512,2048]{1,0:T(8,128)(4,1)S(1)} %broadcast_compare_fusion.5, pred[]{:T(512)S(6)} %compare.3, ...), kind=kOutput, calls=%fused_computation.23.clone.1 | convolution fusion | flops 832045056 | bytes 32911364 | tf_op jit(solution)/shard_map/while/body/eval_jaxpr/hqk,qhd->khd/dot_general | solution.py:163
  489.2 18.1 %multiply_reduce_fusion.3 = (f32[6,512]{1,0:T(8,128)S(1)}, f32[6,512,2048]{2,1,0:T(8,128)}) fusion(f32[6,512,2048]{2,1,0:T(8,128)} %fusion.140, f32[6,512]{1,0:T(8,128)S(1)} %dynamic-slice_bitcast_fusion.2, pred[512,2048]{1,0:T(8,128)(4,1)S(1)} %broadcast_compare_fusion.5, bf16[2048,6,64]{0,2,1:T(8,128)(2,1)} %get-tuple-element.508, ...), kind=kOutput, calls=%fused_computation.18.clone.1 | convolution fusion | flops 836760576 | bytes 53370884 | tf_op jit(solution)/shard_map/while/body/eval_jaxpr/qhd,khd->hqk/dot_general | solution.py:169
  507.3 21.3 %multiply_convert_fusion.3 = bf16[6,512,2048]{2,1,0:T(8,128)(2,1)} fusion(f32[6,512,2048]{2,1,0:T(8,128)} %get-tuple-element.443, f32[6,512,2048]{2,1,0:T(8,128)} %fusion.140, f32[6,512]{1,0:T(8,128)S(1)} %get-tuple-element.444, f32[6,512]{1,0:T(8,128)S(1)} %dynamic-slice_bitcast_fusion.2, pred[512,2048]{1,0:T(8,128)(4,1)S(1)} %broadcast_compare_fusion.5), kind=kLoop, calls=%fused_computation.17.clone.1 | loop fusion | flops 37748736 | bytes 63987712 | tf_op jit(solution)/shard_map/while/body/eval_jaxpr/convert_element_type | solution.py:173
  528.6 9.3 fusion.141
  537.8 9.6 bitcast_add_fusion.4
  548.1 11.0 fusion.140
  559.1 13.7 %bitcast_add_fusion.5 = f32[2048,6,64]{0,2,1:T(8,128)} fusion(f32[2048,6,64]{0,2,1:T(8,128)} %get-tuple-element.487, f32[6,512,2048]{2,1,0:T(8,128)} %fusion.140, f32[6,512]{1,0:T(8,128)S(1)} %dynamic-slice_bitcast_fusion.2, pred[512,2048]{1,0:T(8,128)(4,1)S(1)} %broadcast_compare_fusion.5, pred[]{:T(512)S(6)} %compare.3, ...), kind=kOutput, calls=%fused_computation.23.clone.1 | convolution fusion | flops 832045056 | bytes 32911364 | tf_op jit(solution)/shard_map/while/body/eval_jaxpr/hqk,qhd->khd/dot_general | solution.py:163
  572.8 18.1 %multiply_reduce_fusion.3 = (f32[6,512]{1,0:T(8,128)S(1)}, f32[6,512,2048]{2,1,0:T(8,128)}) fusion(f32[6,512,2048]{2,1,0:T(8,128)} %fusion.140, f32[6,512]{1,0:T(8,128)S(1)} %dynamic-slice_bitcast_fusion.2, pred[512,2048]{1,0:T(8,128)(4,1)S(1)} %broadcast_compare_fusion.5, bf16[2048,6,64]{0,2,1:T(8,128)(2,1)} %get-tuple-element.508, ...), kind=kOutput, calls=%fused_computation.18.clone.1 | convolution fusion | flops 836760576 | bytes 53370884 | tf_op jit(solution)/shard_map/while/body/eval_jaxpr/qhd,khd->hqk/dot_general | solution.py:169
  590.9 21.3 %multiply_convert_fusion.3 = bf16[6,512,2048]{2,1,0:T(8,128)(2,1)} fusion(f32[6,512,2048]{2,1,0:T(8,128)} %get-tuple-element.443, f32[6,512,2048]{2,1,0:T(8,128)} %fusion.140, f32[6,512]{1,0:T(8,128)S(1)} %get-tuple-element.444, f32[6,512]{1,0:T(8,128)S(1)} %dynamic-slice_bitcast_fusion.2, pred[512,2048]{1,0:T(8,128)(4,1)S(1)} %broadcast_compare_fusion.5), kind=kLoop, calls=%fused_computation.17.clone.1 | loop fusion | flops 37748736 | bytes 63987712 | tf_op jit(solution)/shard_map/while/body/eval_jaxpr/convert_element_type | solution.py:173
  612.2 9.3 fusion.141
  621.4 9.6 bitcast_add_fusion.4
  631.7 11.0 fusion.140
  642.7 13.7 %bitcast_add_fusion.5 = f32[2048,6,64]{0,2,1:T(8,128)} fusion(f32[2048,6,64]{0,2,1:T(8,128)} %get-tuple-element.487, f32[6,512,2048]{2,1,0:T(8,128)} %fusion.140, f32[6,512]{1,0:T(8,128)S(1)} %dynamic-slice_bitcast_fusion.2, pred[512,2048]{1,0:T(8,128)(4,1)S(1)} %broadcast_compare_fusion.5, pred[]{:T(512)S(6)} %compare.3, ...), kind=kOutput, calls=%fused_computation.23.clone.1 | convolution fusion | flops 832045056 | bytes 32911364 | tf_op jit(solution)/shard_map/while/body/eval_jaxpr/hqk,qhd->khd/dot_general | solution.py:163
  656.4 18.1 %multiply_reduce_fusion.3 = (f32[6,512]{1,0:T(8,128)S(1)}, f32[6,512,2048]{2,1,0:T(8,128)}) fusion(f32[6,512,2048]{2,1,0:T(8,128)} %fusion.140, f32[6,512]{1,0:T(8,128)S(1)} %dynamic-slice_bitcast_fusion.2, pred[512,2048]{1,0:T(8,128)(4,1)S(1)} %broadcast_compare_fusion.5, bf16[2048,6,64]{0,2,1:T(8,128)(2,1)} %get-tuple-element.508, ...), kind=kOutput, calls=%fused_computation.18.clone.1 | convolution fusion | flops 836760576 | bytes 53370884 | tf_op jit(solution)/shard_map/while/body/eval_jaxpr/qhd,khd->hqk/dot_general | solution.py:169
  674.5 21.3 %multiply_convert_fusion.3 = bf16[6,512,2048]{2,1,0:T(8,128)(2,1)} fusion(f32[6,512,2048]{2,1,0:T(8,128)} %get-tuple-element.443, f32[6,512,2048]{2,1,0:T(8,128)} %fusion.140, f32[6,512]{1,0:T(8,128)S(1)} %get-tuple-element.444, f32[6,512]{1,0:T(8,128)S(1)} %dynamic-slice_bitcast_fusion.2, pred[512,2048]{1,0:T(8,128)(4,1)S(1)} %broadcast_compare_fusion.5), kind=kLoop, calls=%fused_computation.17.clone.1 | loop fusion | flops 37748736 | bytes 63987712 | tf_op jit(solution)/shard_map/while/body/eval_jaxpr/convert_element_type | solution.py:173
  695.8 9.3 fusion.141
  705.0 9.6 bitcast_add_fusion.4
  715.0 3.8 copy.52
  732.9 8.9 bitcast_convert_fusion
  741.9 9.8 fusion.81
  751.7 9.1 fusion.82
  764.5 5.8 fusion.66
  772.7 81.2 %all-reduce.1 = (f32[2,384]{1,0:T(2,128)}, f32[1536]{0:T(1024)}) all-reduce(f32[2,384]{1,0:T(2,128)S(1)} %pad_maximum_fusion.6, f32[1536]{0:T(1024)S(1)} %copy-done.38), channel_id=1, replica_groups=mesh['dp'=16,'mp'=2] {'dp'}, use_global_device_ids=true, to_apply=%region_38.39 | all-reduce | flops 2304 | bytes 18432 | tf_op jit(solution)/shard_map/psum | solution.py:234
  858.7 41.5 %all-reduce = (f32[2,768]{1,0:T(2,128)}, f32[4,768]{1,0:T(4,128)}) all-reduce(f32[2,768]{1,0:T(2,128)S(1)} %pad_maximum_fusion.5, f32[4,768]{1,0:T(4,128)S(1)} %pad_maximum_fusion.3), channel_id=1, replica_groups=mesh['dp'=16,'mp'=2] {'dp','mp'}, use_global_device_ids=true, to_apply=%region_29.30 | all-reduce | flops 4608 | bytes 36864 | tf_op jit(solution)/shard_map/psum | solution.py:220
  900.1 4.1 add_add_fusion.2
  904.2 267.0 %all-reduce.5.cloned.1.call-done = (f32[3,768,384]{1,2,0:T(8,128)}, f32[384,768]{1,0:T(8,128)}, f32[768,1536]{1,0:T(8,128)}, f32[1536,768]{1,0:T(8,128)}) async-done(((f32[3,768,384]{1,2,0:T(8,128)}, f32[384,768]{1,0:T(8,128)}, f32[768,1536]{1,0:T(8,128)}, f32[1536,768]{1,0:T(8,128)}), (f32[3,768,384]{1,2,0:T(8,128)}, f32[384,768]{1,0:T(8,128)}, f32[768,1536]{1,0:T(8,128)}, ...) | async-done | bytes 14155792 | tf_op jit(solution)/shard_map/psum | solution.py:234
  1171.3 5.2 copy.57
  1177.5 5.5 copy.92
  (237 shorter events, 87.9 us)
Async XLA Ops:
  7.2 275.3 %copy-start = (bf16[768,1536]{1,0:T(8,128)(2,1)S(1)}, bf16[768,1536]{1,0:T(8,128)(2,1)}, u32[]{:S(2)}) copy-start(bf16[768,1536]{1,0:T(8,128)(2,1)} %param.25) | copy-start | bytes 7077892
  7.2 4.6 copy-start.39
  7.2 5.2 copy-start.37
  7.2 22.6 %all-gather.5.cloned.1.call-start = ((), (), s32[]{:S(2)}) async-start(), calls=%async_computation.4 | async-start | bytes 4718592 | tf_op jit(solution)/shard_map/all_gather | solution.py:78
  7.3 5.8 copy-start.3
  9.1 3.9 copy-start.22
  9.1 5.8 copy-start.41
  9.1 6.3 copy-start.40
  11.8 1.3 copy-start.27
  14.8 211.6 %reduce-scatter.5.cloned.1.call-start = ((), (), s32[]{:S(2)}) async-start(), calls=%async_computation.5 | async-start | bytes 4718592 | tf_op jit(solution)/shard_map/reduce_scatter | solution.py:107
  61.6 12.1 %copy-start.7 = (bf16[2048,6,64]{0,2,1:T(8,128)(2,1)S(1)}, bf16[2048,6,64]{0,2,1:T(8,128)(2,1)}, u32[]{:S(2)}) copy-start(bf16[2048,6,64]{0,2,1:T(8,128)(2,1)} %get-tuple-element.470) | copy-start | bytes 4718596 | tf_op jit(solution)/shard_map/while
  61.6 12.1 %copy-start.13 = (bf16[4,512,6,64]{1,3,2,0:T(8,128)(2,1)S(1)}, bf16[4,512,6,64]{1,3,2,0:T(8,128)(2,1)}, u32[]{:S(2)}) copy-start(bf16[4,512,6,64]{1,3,2,0:T(8,128)(2,1)} %get-tuple-element.455) | copy-start | bytes 4718596 | tf_op jit(solution)/shard_map/while
  85.4 1.1 copy-start.14
  101.5 12.1 %copy-start.7 = (bf16[2048,6,64]{0,2,1:T(8,128)(2,1)S(1)}, bf16[2048,6,64]{0,2,1:T(8,128)(2,1)}, u32[]{:S(2)}) copy-start(bf16[2048,6,64]{0,2,1:T(8,128)(2,1)} %get-tuple-element.470) | copy-start | bytes 4718596 | tf_op jit(solution)/shard_map/while
  101.5 12.1 %copy-start.13 = (bf16[4,512,6,64]{1,3,2,0:T(8,128)(2,1)S(1)}, bf16[4,512,6,64]{1,3,2,0:T(8,128)(2,1)}, u32[]{:S(2)}) copy-start(bf16[4,512,6,64]{1,3,2,0:T(8,128)(2,1)} %get-tuple-element.455) | copy-start | bytes 4718596 | tf_op jit(solution)/shard_map/while
  125.2 1.1 copy-start.14
  141.3 12.1 %copy-start.7 = (bf16[2048,6,64]{0,2,1:T(8,128)(2,1)S(1)}, bf16[2048,6,64]{0,2,1:T(8,128)(2,1)}, u32[]{:S(2)}) copy-start(bf16[2048,6,64]{0,2,1:T(8,128)(2,1)} %get-tuple-element.470) | copy-start | bytes 4718596 | tf_op jit(solution)/shard_map/while
  141.3 12.1 %copy-start.13 = (bf16[4,512,6,64]{1,3,2,0:T(8,128)(2,1)S(1)}, bf16[4,512,6,64]{1,3,2,0:T(8,128)(2,1)}, u32[]{:S(2)}) copy-start(bf16[4,512,6,64]{1,3,2,0:T(8,128)(2,1)} %get-tuple-element.455) | copy-start | bytes 4718596 | tf_op jit(solution)/shard_map/while
  165.1 1.1 copy-start.14
  181.2 12.1 %copy-start.7 = (bf16[2048,6,64]{0,2,1:T(8,128)(2,1)S(1)}, bf16[2048,6,64]{0,2,1:T(8,128)(2,1)}, u32[]{:S(2)}) copy-start(bf16[2048,6,64]{0,2,1:T(8,128)(2,1)} %get-tuple-element.470) | copy-start | bytes 4718596 | tf_op jit(solution)/shard_map/while
  181.2 12.1 %copy-start.13 = (bf16[4,512,6,64]{1,3,2,0:T(8,128)(2,1)S(1)}, bf16[4,512,6,64]{1,3,2,0:T(8,128)(2,1)}, u32[]{:S(2)}) copy-start(bf16[4,512,6,64]{1,3,2,0:T(8,128)(2,1)} %get-tuple-element.455) | copy-start | bytes 4718596 | tf_op jit(solution)/shard_map/while
  205.0 1.1 copy-start.14
  206.3 4.3 copy-start.47
  209.4 1.2 copy-start.15
  214.1 12.3 %copy-start.21 = (f32[768]{0:T(1024)S(1)}, f32[768]{0:T(1024)}, u32[]{:S(2)}) copy-start(f32[768]{0:T(1024)} %get-tuple-element.249) | copy-start | bytes 9220
  214.2 68.3 %all-gather.7.cloned.1.call-start = ((), (), s32[]{:S(2)}) async-start(), calls=%async_computation.6 | async-start | bytes 4718592 | tf_op jit(solution)/shard_map/all_gather | solution.py:115
  226.4 2.6 copy-start.4
  226.4 2.8 copy-start.8
  226.4 3.7 copy-start.26
  226.4 3.7 copy-start.34
  230.1 2.8 copy-start.42
  232.2 50.3 %copy-start.48 = (f32[1536]{0:T(1024)S(1)}, f32[1536]{0:T(1024)}, u32[]{:S(2)}) copy-start(f32[1536]{0:T(1024)} %param.26) | copy-start | bytes 18436
  232.2 64.0 %all-gather.9.cloned.1.call-start = ((), (), s32[]{:S(2)}) async-start(), calls=%async_computation.8 | async-start | bytes 4718592 | tf_op jit(solution)/shard_map/all_gather | solution.py:128
  282.4 54.2 %reduce-scatter.9.cloned.1.call-start = ((), (), s32[]{:S(2)}) async-start(), calls=%async_computation.9 | async-start | bytes 4718592 | tf_op jit(solution)/shard_map/reduce_scatter | solution.py:139
  315.6 2.6 copy-start.49
  324.6 1.7 copy-start.46
  324.7 21.7 %reduce-scatter.7.cloned.1.call-start = ((), (), s32[]{:S(2)}) async-start(), calls=%async_computation.7 | async-start | bytes 4718592 | tf_op jit(solution)/shard_map/reduce_scatter | solution.py:120
  335.9 1.4 copy-start.5
  336.0 32.4 %all-gather.11.cloned.1.call-start = ((), (), s32[]{:S(2)}) async-start(), calls=%async_computation.10 | async-start | bytes 4718592 | tf_op jit(solution)/shard_map/all_gather | solution.py:149
  337.4 3.9 copy-start.12
  341.2 5.1 copy-start.31
  351.9 1.7 copy-start.9
  354.9 499.0 %reduce-scatter.11.cloned.1.call-start = ((), (), s32[]{:S(2)}) async-start(), calls=%async_computation.11 | async-start | bytes 4718592 | tf_op jit(solution)/shard_map/reduce_scatter | solution.py:210
  377.3 4.4 copy-start.2
  721.6 5.0 copy-start.10
  741.8 429.4 %all-reduce.5.cloned.1.call-start = ((), (), s32[]{:S(2)}) async-start(), calls=%async_computation.12 | async-start | bytes 28311552 | tf_op jit(solution)/shard_map/psum | solution.py:234
  741.9 9.8 copy-start.44
  751.7 9.1 copy-start.16
  751.7 9.1 copy-start.45
  760.7 2.4 copy-start.17
  760.8 2.4 copy-start.18
  760.8 2.4 copy-start.19
  760.8 3.7 copy-start.43
  770.3 2.5 copy-start.38
  770.3 83.7 %copy-start.6 = (bf16[1024,768]{1,0:T(8,128)(2,1)S(1)}, bf16[1024,768]{1,0:T(8,128)(2,1)}, u32[]{:S(2)}) copy-start(bf16[1024,768]{1,0:T(8,128)(2,1)} %param.16) | copy-start | bytes 4718596
  770.3 83.7 %copy-start.23 = (f32[1024]{0:T(1024)S(1)}, f32[1024]{0:T(1024)}, u32[]{:S(2)}) copy-start(f32[1024]{0:T(1024)} %copy-done.22) | copy-start | bytes 12292
  770.3 83.6 %copy-start.25 = (f32[768]{0:T(1024)S(1)}, f32[768]{0:T(1024)}, u32[]{:S(2)}) copy-start(f32[768]{0:T(1024)} %copy-done.24) | copy-start | bytes 9220
  770.3 86.3 %copy-start.30 = (f32[1024]{0:T(1024)S(1)}, f32[1024]{0:T(1024)}, u32[]{:S(2)}) copy-start(f32[1024]{0:T(1024)} %copy-done.29) | copy-start | bytes 12292
  770.3 86.3 %copy-start.28 = (f32[1024]{0:T(1024)S(1)}, f32[1024]{0:T(1024)}, u32[]{:S(2)}) copy-start(f32[1024]{0:T(1024)} %copy-done.27) | copy-start | bytes 12292
  854.0 2.7 copy-start.11
  1171.3 5.3 copy-start.20
  1176.5 6.5 slice-start
  1177.5 5.5 slice-start.1
  1177.5 7.7 copy-start.1
  (6 other events, 4.0 us)
Sparse Core Ops, SparseCore 0:
  15.0 14.8 all-gather.4
  214.3 12.0 reduce-scatter.4
  232.3 13.3 all-gather.6
  282.5 7.9 all-gather.8
  324.8 6.7 reduce-scatter.8
  336.1 10.2 reduce-scatter.6
  355.1 13.2 all-gather.10
  742.0 12.0 reduce-scatter.10
  770.5 400.7 all-reduce.4
where the time goes:
time: 1200 us; the launch traced here: 1190 us
  matrix products  448 us (37%)
  waiting for transfers between devices  308 us (26%)
  other arithmetic  188 us (16%)
  blocking collectives  165 us (14%)
  local copies, waits for them, and re-layouts  65.3 us (5%)
  between operations  15.9 us (1%)
    psum x1, waiting for transfers between devices, local(): lax.psum((grad_qkv, grad_qv_bias, grad_out, grad_fc1, grad_bfc1, grad_fc2...  267 us
    dot_general x8, matrix products, score_block(): jnp.einsum('qhd,khd->hqk', query_block, keys_all, preferred_element_type=...  101 us
    convert_element_type x4, other arithmetic, backward_block(): grad_scores = grad_scores.astype(jnp.bfloat16)  85.1 us
    psum x1, blocking collectives, local(): lax.psum((grad_qkv, grad_qv_bias, grad_out, grad_fc1, grad_bfc1, grad_fc2...  81.2 us
    dot_general x4, matrix products, backward_block(): jnp.einsum('qhd,khd->hqk', grad_block, values_all, preferred_element_type...  72.3 us
    dot_general x4, matrix products, backward_block(): jnp.einsum('hqk,qhd->khd', probs.astype(jnp.bfloat16), grad_block, prefer...  53.8 us
    reduce_sum x4, other arithmetic, forward_block(): total = jnp.sum(exponent, axis=-1, keepdims=True)  48.4 us
    dot_general x4, matrix products, forward_block(): jnp.einsum('hqk,khd->qhd', weights, values_all, preferred_element_type=jn...  46.6 us
  transfers between devices with their start and end apart: 9, of which 5 were waited for; matrix products, arithmetic and copies ran while one was open for 6% of the time, Pallas kernels for 0%

commit v1 on v0

--- a/solution.py
+++ b/solution.py
@@ -61,7 +61,7 @@
     segment, row_length = image_rows(image_lengths[0], row_count)
     images = jnp.sum((image_lengths[0] > 0).astype(jnp.float32))
     member = (group_of_block[0] == jnp.arange(GROUPS, dtype=jnp.int32)).astype(jnp.float32)
-    group_images = lax.psum(member * images, "dp")
+    group_images = jnp.sum(lax.all_gather(member * images, axis_name="dp"), axis=0)
     group_roots = jnp.sqrt(group_images)
     factor = jnp.sum(group_images) / (group_roots * jnp.sum(group_roots))
     block_factor = jnp.sum(member * factor)

time: 1200 us -> 1200 us (level)
    psum x1 -> x0, blocking collectives: 41.9 us -> none  [local(): group_images = lax.psum(member * images, 'dp')]
    all_gather x0 -> x1, blocking collectives: none -> 40.6 us  [local(): lax.all_gather(member * images, axis_name='dp')]
where the time goes in v1:
time: 1200 us; the launch traced here: 1190 us
  matrix products  448 us (37%)
  waiting for transfers between devices  308 us (26%)
  other arithmetic  189 us (16%)
  blocking collectives  163 us (14%)
  local copies, waits for them, and re-layouts  65.3 us (5%)
  between operations  15.9 us (1%)
    psum x1, waiting for transfers between devices, local(): lax.psum((grad_qkv, grad_qv_bias, grad_out, grad_fc1, grad_bfc1, grad_fc2...  267 us
    dot_general x8, matrix products, score_block(): jnp.einsum('qhd,khd->hqk', query_block, keys_all, preferred_element_type=...  101 us
    convert_element_type x4, other arithmetic, backward_block(): grad_scores = grad_scores.astype(jnp.bfloat16)  85.1 us
    psum x1, blocking collectives, local(): lax.psum((grad_qkv, grad_qv_bias, grad_out, grad_fc1, grad_bfc1, grad_fc2...  81.2 us
    dot_general x4, matrix products, backward_block(): jnp.einsum('qhd,khd->hqk', grad_block, values_all, preferred_element_type...  72.3 us
    dot_general x4, matrix products, backward_block(): jnp.einsum('hqk,qhd->khd', probs.astype(jnp.bfloat16), grad_block, prefer...  53.8 us
    reduce_sum x4, other arithmetic, forward_block(): total = jnp.sum(exponent, axis=-1, keepdims=True)  48.4 us
    dot_general x4, matrix products, forward_block(): jnp.einsum('hqk,khd->qhd', weights, values_all, preferred_element_type=jn...  46.6 us
  transfers between devices with their start and end apart: 9, of which 5 were waited for; matrix products, arithmetic and copies ran while one was open for 6% of the time, Pallas kernels for 0%

profile of v1, /device:TPU:0, one launch (start us, length us, event | category | flops | bytes accessed | tf_op | source)
XLA Modules:
  0.0 1191.3 jit_solution(15593499263766875377)
XLA Ops:
  15.5 14.2 %all-gather.6.cloned.1.call-done = bf16[2048,768]{1,0:T(8,128)(2,1)} async-done(((bf16[1024,768]{1,0:T(8,128)(2,1)}), bf16[2048,768]{1,0:T(8,128)(2,1)}) %all-gather.6.cloned.1.call-update) | async-done | bytes 3145744 | tf_op jit(solution)/shard_map/all_gather | solution.py:78
  29.8 6.3 fusion.45
  38.4 4.0 reshape_squeeze.3
  46.6 159.6 %while.27 = (s32[]{:T(128)}, bf16[4,512,6,64]{1,3,2,0:T(8,128)(2,1)}, f32[4,6,512]{2,1,0:T(8,128)S(1)}, s32[4,512]{1,0:T(4,128)S(1)}, s32[2048]{0:T(1024)S(1)}, ...) while((s32[]{:T(128)}, ...), condition=%wide.region_7.8_spmd, body=%wide.region_4.7_spmd.sunk | while | flops 1687155712 | bytes 103024832 | solution.py:104
  47.3 14.3 %fusion.129 = (f32[6,512]{1,0:T(8,128)S(1)}, f32[6,512,2048]{2,1,0:T(8,128)}) fusion(pred[512,2048]{1,0:T(8,128)(4,1)S(1)} %broadcast_compare_fusion.4, bf16[2048,6,64]{0,2,1:T(8,128)(2,1)} %get-tuple-element.500, bf16[4,512,6,64]{1,3,2,0:T(8,128)(2,1)} %get-tuple-element.499, s32[]{:T(128)S(6)} %copy.80), kind=kOutput, calls=%fused_computation.3.clone.1 | convolution fusion | flops 824177664 | bytes 28192772 | tf_op jit(solution)/shard_map/while/body/eval_jaxpr/qhd,khd->hqk/dot_general | solution.py:38
  61.6 12.1 %fusion.130 = f32[6,512]{1,0:T(8,128)S(1)} fusion(f32[6,512,2048]{2,1,0:T(8,128)} %get-tuple-element.461, f32[6,512]{1,0:T(8,128)S(1)} %get-tuple-element.462, pred[512,2048]{1,0:T(8,128)(4,1)S(1)} %broadcast_compare_fusion.4), kind=kLoop, calls=%fused_computation.4.clone.1 | loop fusion | flops 25162752 | bytes 26238976 | tf_op jit(solution)/shard_map/while/body/eval_jaxpr/reduce_sum | solution.py:97
  73.7 11.6 fusion.131
  87.2 14.3 %fusion.129 = (f32[6,512]{1,0:T(8,128)S(1)}, f32[6,512,2048]{2,1,0:T(8,128)}) fusion(pred[512,2048]{1,0:T(8,128)(4,1)S(1)} %broadcast_compare_fusion.4, bf16[2048,6,64]{0,2,1:T(8,128)(2,1)} %get-tuple-element.500, bf16[4,512,6,64]{1,3,2,0:T(8,128)(2,1)} %get-tuple-element.499, s32[]{:T(128)S(6)} %copy.80), kind=kOutput, calls=%fused_computation.3.clone.1 | convolution fusion | flops 824177664 | bytes 28192772 | tf_op jit(solution)/shard_map/while/body/eval_jaxpr/qhd,khd->hqk/dot_general | solution.py:38
  101.4 12.1 %fusion.130 = f32[6,512]{1,0:T(8,128)S(1)} fusion(f32[6,512,2048]{2,1,0:T(8,128)} %get-tuple-element.461, f32[6,512]{1,0:T(8,128)S(1)} %get-tuple-element.462, pred[512,2048]{1,0:T(8,128)(4,1)S(1)} %broadcast_compare_fusion.4), kind=kLoop, calls=%fused_computation.4.clone.1 | loop fusion | flops 25162752 | bytes 26238976 | tf_op jit(solution)/shard_map/while/body/eval_jaxpr/reduce_sum | solution.py:97
  113.6 11.6 fusion.131
  127.0 14.3 %fusion.129 = (f32[6,512]{1,0:T(8,128)S(1)}, f32[6,512,2048]{2,1,0:T(8,128)}) fusion(pred[512,2048]{1,0:T(8,128)(4,1)S(1)} %broadcast_compare_fusion.4, bf16[2048,6,64]{0,2,1:T(8,128)(2,1)} %get-tuple-element.500, bf16[4,512,6,64]{1,3,2,0:T(8,128)(2,1)} %get-tuple-element.499, s32[]{:T(128)S(6)} %copy.80), kind=kOutput, calls=%fused_computation.3.clone.1 | convolution fusion | flops 824177664 | bytes 28192772 | tf_op jit(solution)/shard_map/while/body/eval_jaxpr/qhd,khd->hqk/dot_general | solution.py:38
  141.3 12.1 %fusion.130 = f32[6,512]{1,0:T(8,128)S(1)} fusion(f32[6,512,2048]{2,1,0:T(8,128)} %get-tuple-element.461, f32[6,512]{1,0:T(8,128)S(1)} %get-tuple-element.462, pred[512,2048]{1,0:T(8,128)(4,1)S(1)} %broadcast_compare_fusion.4), kind=kLoop, calls=%fused_computation.4.clone.1 | loop fusion | flops 25162752 | bytes 26238976 | tf_op jit(solution)/shard_map/while/body/eval_jaxpr/reduce_sum | solution.py:97
  153.4 11.6 fusion.131
  166.9 14.3 %fusion.129 = (f32[6,512]{1,0:T(8,128)S(1)}, f32[6,512,2048]{2,1,0:T(8,128)}) fusion(pred[512,2048]{1,0:T(8,128)(4,1)S(1)} %broadcast_compare_fusion.4, bf16[2048,6,64]{0,2,1:T(8,128)(2,1)} %get-tuple-element.500, bf16[4,512,6,64]{1,3,2,0:T(8,128)(2,1)} %get-tuple-element.499, s32[]{:T(128)S(6)} %copy.80), kind=kOutput, calls=%fused_computation.3.clone.1 | convolution fusion | flops 824177664 | bytes 28192772 | tf_op jit(solution)/shard_map/while/body/eval_jaxpr/qhd,khd->hqk/dot_general | solution.py:38
  181.2 12.1 %fusion.130 = f32[6,512]{1,0:T(8,128)S(1)} fusion(f32[6,512,2048]{2,1,0:T(8,128)} %get-tuple-element.461, f32[6,512]{1,0:T(8,128)S(1)} %get-tuple-element.462, pred[512,2048]{1,0:T(8,128)(4,1)S(1)} %broadcast_compare_fusion.4), kind=kLoop, calls=%fused_computation.4.clone.1 | loop fusion | flops 25162752 | bytes 26238976 | tf_op jit(solution)/shard_map/while/body/eval_jaxpr/reduce_sum | solution.py:97
  193.3 11.6 fusion.131
  210.6 3.5 convolution_convert_fusion
  214.2 12.2 %reduce-scatter.5.cloned.1.call-done = bf16[1024,768]{1,0:T(8,128)(2,1)} async-done(((bf16[2048,768]{1,0:T(8,128)(2,1)}), bf16[1024,768]{1,0:T(8,128)(2,1)}) %reduce-scatter.5.cloned.1.call-update) | async-done | bytes 1572880 | tf_op jit(solution)/shard_map/reduce_scatter | solution.py:107
  234.1 40.6 %all-gather = f32[16,1,3]{2,1,0:T(1,128)S(1)} all-gather(f32[1,1,3]{2,1,0:T(1,128)S(1)} %fusion.71), channel_id=1, replica_groups=mesh['dp'=16,'mp'=2] {'dp'}, dimensions={0}, use_global_device_ids=true | all-gather | bytes 204 | tf_op jit(solution)/shard_map/all_gather | solution.py:64
  281.7 13.7 %multiply_convert_fusion.1 = (bf16[2048,1536]{1,0:T(8,128)(2,1)}, f32[2048,1536]{1,0:T(8,128)}) fusion(f32[1536]{0:T(1024)S(1)} %copy-done.48, bf16[2048,768]{1,0:T(8,128)(2,1)} %all-gather.8.cloned.1.call-done, bf16[768,1536]{1,0:T(8,128)(2,1)S(1)} %copy-done), kind=kOutput, calls=%fused_computation.58 | convolution fusion | flops 4863295488 | bytes 24385536 | tf_op jit(solution)/shard_map/dot_general | solution.py:116
  295.4 19.5 %convert_reduce_fusion = (f32[1536]{0:T(1024)}, bf16[2048,1536]{1,0:T(8,128)(2,1)S(1)}) fusion(bf16[2048,768]{1,0:T(8,128)(2,1)} %all-gather.10.cloned.1.call-done, bf16[1536,768]{1,0:T(8,128)(2,1)} %param.27, f32[2048,1536]{1,0:T(8,128)} %get-tuple-element.347, f32[1536]{0:T(1024)S(1)} %copy-done.48), kind=kOutput, calls=%fused_computation.57 | convolution fusion | flops 4916771328 | bytes 24391680 | tf_op jit(solution)/shard_map/rd,fd->rf/dot_general | solution.py:132
  317.5 6.4 convolution_convert_fusion.1
  325.6 9.7 convolution_convert_fusion.2
  336.6 3.9 convert_reduce_fusion.2
  340.5 4.2 fusion.56
  345.6 5.6 fusion.78
  354.3 13.4 %all-gather.12.cloned.1.call-done = bf16[2048,768]{1,0:T(8,128)(2,1)} async-done(((bf16[1024,768]{1,0:T(8,128)(2,1)}), bf16[2048,768]{1,0:T(8,128)(2,1)}) %all-gather.12.cloned.1.call-update) | async-done | bytes 3145744 | tf_op jit(solution)/shard_map/all_gather | solution.py:149
  367.6 4.9 convolution_convert_fusion.3
  381.0 333.3 %while.28 = (s32[]{:T(128)}, f32[2048,6,64]{0,2,1:T(8,128)}, f32[2048,6,64]{0,2,1:T(8,128)}, bf16[4,512,6,64]{1,3,2,0:T(8,128)(2,1)}, bf16[4,512,6,64]{1,3,2,0:T...) while((s32[]{:T(128)}, f32[2048,6,64]{0,2,1:T(8,128)}, ...), condition=%wide.region_23.24_spmd.clone, body=%wide.region_21.23_spmd.clone.sunk | while | flops 4126077952 | bytes 212699312 | solution.py:188
  381.9 11.0 fusion.141
  392.9 12.8 %bitcast_add_fusion.5 = f32[2048,6,64]{0,2,1:T(8,128)} fusion(f32[2048,6,64]{0,2,1:T(8,128)} %get-tuple-element.518, f32[6,512,2048]{2,1,0:T(8,128)} %fusion.141, f32[6,512]{1,0:T(8,128)S(1)} %dynamic-slice_bitcast_fusion.2, pred[512,2048]{1,0:T(8,128)(4,1)S(1)} %broadcast_compare_fusion.5, pred[]{:T(512)S(6)} %compare.3, ...), kind=kOutput, calls=%fused_computation.23.clone.1 | convolution fusion | flops 832045056 | bytes 32911364 | tf_op jit(solution)/shard_map/while/body/eval_jaxpr/hqk,qhd->khd/dot_general | solution.py:163
  405.8 18.1 %multiply_reduce_fusion.3 = (f32[6,512]{1,0:T(8,128)S(1)}, f32[6,512,2048]{2,1,0:T(8,128)}) fusion(f32[6,512,2048]{2,1,0:T(8,128)} %fusion.141, f32[6,512]{1,0:T(8,128)S(1)} %dynamic-slice_bitcast_fusion.2, pred[512,2048]{1,0:T(8,128)(4,1)S(1)} %broadcast_compare_fusion.5, bf16[2048,6,64]{0,2,1:T(8,128)(2,1)} %get-tuple-element.539, ...), kind=kOutput, calls=%fused_computation.18.clone.1 | convolution fusion | flops 836760576 | bytes 53370884 | tf_op jit(solution)/shard_map/while/body/eval_jaxpr/qhd,khd->hqk/dot_general | solution.py:169
  423.8 21.3 %multiply_convert_fusion.3 = bf16[6,512,2048]{2,1,0:T(8,128)(2,1)} fusion(f32[6,512,2048]{2,1,0:T(8,128)} %get-tuple-element.474, f32[6,512,2048]{2,1,0:T(8,128)} %fusion.141, f32[6,512]{1,0:T(8,128)S(1)} %get-tuple-element.475, f32[6,512]{1,0:T(8,128)S(1)} %dynamic-slice_bitcast_fusion.2, pred[512,2048]{1,0:T(8,128)(4,1)S(1)} %broadcast_compare_fusion.5), kind=kLoop, calls=%fused_computation.17.clone.1 | loop fusion | flops 37748736 | bytes 63987712 | tf_op jit(solution)/shard_map/while/body/eval_jaxpr/convert_element_type | solution.py:173
  445.1 9.3 fusion.142
  454.4 8.7 bitcast_add_fusion.4
  463.8 11.0 fusion.141
  474.8 13.7 %bitcast_add_fusion.5 = f32[2048,6,64]{0,2,1:T(8,128)} fusion(f32[2048,6,64]{0,2,1:T(8,128)} %get-tuple-element.518, f32[6,512,2048]{2,1,0:T(8,128)} %fusion.141, f32[6,512]{1,0:T(8,128)S(1)} %dynamic-slice_bitcast_fusion.2, pred[512,2048]{1,0:T(8,128)(4,1)S(1)} %broadcast_compare_fusion.5, pred[]{:T(512)S(6)} %compare.3, ...), kind=kOutput, calls=%fused_computation.23.clone.1 | convolution fusion | flops 832045056 | bytes 32911364 | tf_op jit(solution)/shard_map/while/body/eval_jaxpr/hqk,qhd->khd/dot_general | solution.py:163
  488.5 18.1 %multiply_reduce_fusion.3 = (f32[6,512]{1,0:T(8,128)S(1)}, f32[6,512,2048]{2,1,0:T(8,128)}) fusion(f32[6,512,2048]{2,1,0:T(8,128)} %fusion.141, f32[6,512]{1,0:T(8,128)S(1)} %dynamic-slice_bitcast_fusion.2, pred[512,2048]{1,0:T(8,128)(4,1)S(1)} %broadcast_compare_fusion.5, bf16[2048,6,64]{0,2,1:T(8,128)(2,1)} %get-tuple-element.539, ...), kind=kOutput, calls=%fused_computation.18.clone.1 | convolution fusion | flops 836760576 | bytes 53370884 | tf_op jit(solution)/shard_map/while/body/eval_jaxpr/qhd,khd->hqk/dot_general | solution.py:169
  506.6 21.3 %multiply_convert_fusion.3 = bf16[6,512,2048]{2,1,0:T(8,128)(2,1)} fusion(f32[6,512,2048]{2,1,0:T(8,128)} %get-tuple-element.474, f32[6,512,2048]{2,1,0:T(8,128)} %fusion.141, f32[6,512]{1,0:T(8,128)S(1)} %get-tuple-element.475, f32[6,512]{1,0:T(8,128)S(1)} %dynamic-slice_bitcast_fusion.2, pred[512,2048]{1,0:T(8,128)(4,1)S(1)} %broadcast_compare_fusion.5), kind=kLoop, calls=%fused_computation.17.clone.1 | loop fusion | flops 37748736 | bytes 63987712 | tf_op jit(solution)/shard_map/while/body/eval_jaxpr/convert_element_type | solution.py:173
  527.9 9.3 fusion.142
  537.1 9.6 bitcast_add_fusion.4
  547.4 11.0 fusion.141
  558.4 13.7 %bitcast_add_fusion.5 = f32[2048,6,64]{0,2,1:T(8,128)} fusion(f32[2048,6,64]{0,2,1:T(8,128)} %get-tuple-element.518, f32[6,512,2048]{2,1,0:T(8,128)} %fusion.141, f32[6,512]{1,0:T(8,128)S(1)} %dynamic-slice_bitcast_fusion.2, pred[512,2048]{1,0:T(8,128)(4,1)S(1)} %broadcast_compare_fusion.5, pred[]{:T(512)S(6)} %compare.3, ...), kind=kOutput, calls=%fused_computation.23.clone.1 | convolution fusion | flops 832045056 | bytes 32911364 | tf_op jit(solution)/shard_map/while/body/eval_jaxpr/hqk,qhd->khd/dot_general | solution.py:163
  572.1 18.1 %multiply_reduce_fusion.3 = (f32[6,512]{1,0:T(8,128)S(1)}, f32[6,512,2048]{2,1,0:T(8,128)}) fusion(f32[6,512,2048]{2,1,0:T(8,128)} %fusion.141, f32[6,512]{1,0:T(8,128)S(1)} %dynamic-slice_bitcast_fusion.2, pred[512,2048]{1,0:T(8,128)(4,1)S(1)} %broadcast_compare_fusion.5, bf16[2048,6,64]{0,2,1:T(8,128)(2,1)} %get-tuple-element.539, ...), kind=kOutput, calls=%fused_computation.18.clone.1 | convolution fusion | flops 836760576 | bytes 53370884 | tf_op jit(solution)/shard_map/while/body/eval_jaxpr/qhd,khd->hqk/dot_general | solution.py:169
  590.2 21.3 %multiply_convert_fusion.3 = bf16[6,512,2048]{2,1,0:T(8,128)(2,1)} fusion(f32[6,512,2048]{2,1,0:T(8,128)} %get-tuple-element.474, f32[6,512,2048]{2,1,0:T(8,128)} %fusion.141, f32[6,512]{1,0:T(8,128)S(1)} %get-tuple-element.475, f32[6,512]{1,0:T(8,128)S(1)} %dynamic-slice_bitcast_fusion.2, pred[512,2048]{1,0:T(8,128)(4,1)S(1)} %broadcast_compare_fusion.5), kind=kLoop, calls=%fused_computation.17.clone.1 | loop fusion | flops 37748736 | bytes 63987712 | tf_op jit(solution)/shard_map/while/body/eval_jaxpr/convert_element_type | solution.py:173
  611.4 9.3 fusion.142
  620.7 9.6 bitcast_add_fusion.4
  631.0 11.0 fusion.141
  642.0 13.7 %bitcast_add_fusion.5 = f32[2048,6,64]{0,2,1:T(8,128)} fusion(f32[2048,6,64]{0,2,1:T(8,128)} %get-tuple-element.518, f32[6,512,2048]{2,1,0:T(8,128)} %fusion.141, f32[6,512]{1,0:T(8,128)S(1)} %dynamic-slice_bitcast_fusion.2, pred[512,2048]{1,0:T(8,128)(4,1)S(1)} %broadcast_compare_fusion.5, pred[]{:T(512)S(6)} %compare.3, ...), kind=kOutput, calls=%fused_computation.23.clone.1 | convolution fusion | flops 832045056 | bytes 32911364 | tf_op jit(solution)/shard_map/while/body/eval_jaxpr/hqk,qhd->khd/dot_general | solution.py:163
  655.7 18.1 %multiply_reduce_fusion.3 = (f32[6,512]{1,0:T(8,128)S(1)}, f32[6,512,2048]{2,1,0:T(8,128)}) fusion(f32[6,512,2048]{2,1,0:T(8,128)} %fusion.141, f32[6,512]{1,0:T(8,128)S(1)} %dynamic-slice_bitcast_fusion.2, pred[512,2048]{1,0:T(8,128)(4,1)S(1)} %broadcast_compare_fusion.5, bf16[2048,6,64]{0,2,1:T(8,128)(2,1)} %get-tuple-element.539, ...), kind=kOutput, calls=%fused_computation.18.clone.1 | convolution fusion | flops 836760576 | bytes 53370884 | tf_op jit(solution)/shard_map/while/body/eval_jaxpr/qhd,khd->hqk/dot_general | solution.py:169
  673.8 21.3 %multiply_convert_fusion.3 = bf16[6,512,2048]{2,1,0:T(8,128)(2,1)} fusion(f32[6,512,2048]{2,1,0:T(8,128)} %get-tuple-element.474, f32[6,512,2048]{2,1,0:T(8,128)} %fusion.141, f32[6,512]{1,0:T(8,128)S(1)} %get-tuple-element.475, f32[6,512]{1,0:T(8,128)S(1)} %dynamic-slice_bitcast_fusion.2, pred[512,2048]{1,0:T(8,128)(4,1)S(1)} %broadcast_compare_fusion.5), kind=kLoop, calls=%fused_computation.17.clone.1 | loop fusion | flops 37748736 | bytes 63987712 | tf_op jit(solution)/shard_map/while/body/eval_jaxpr/convert_element_type | solution.py:173
  695.0 9.3 fusion.142
  704.3 9.6 bitcast_add_fusion.4
  714.3 3.8 copy.65
  732.2 8.9 bitcast_convert_fusion
  741.2 9.8 fusion.82
  751.0 9.1 fusion.83
  763.8 5.8 fusion.66
  772.0 81.2 %all-reduce.1 = (f32[2,384]{1,0:T(2,128)}, f32[1536]{0:T(1024)}) all-reduce(f32[2,384]{1,0:T(2,128)S(1)} %pad_maximum_fusion.6, f32[1536]{0:T(1024)S(1)} %copy-done.38), channel_id=1, replica_groups=mesh['dp'=16,'mp'=2] {'dp'}, use_global_device_ids=true, to_apply=%region_38.39 | all-reduce | flops 2304 | bytes 18432 | tf_op jit(solution)/shard_map/psum | solution.py:234
  858.0 41.5 %all-reduce = (f32[2,768]{1,0:T(2,128)}, f32[4,768]{1,0:T(4,128)}) all-reduce(f32[2,768]{1,0:T(2,128)S(1)} %pad_maximum_fusion.5, f32[4,768]{1,0:T(4,128)S(1)} %pad_maximum_fusion.3), channel_id=1, replica_groups=mesh['dp'=16,'mp'=2] {'dp','mp'}, use_global_device_ids=true, to_apply=%region_29.30 | all-reduce | flops 4608 | bytes 36864 | tf_op jit(solution)/shard_map/psum | solution.py:220
  899.4 4.1 add_add_fusion.2
  903.5 267.0 %all-reduce.5.cloned.1.call-done = (f32[3,768,384]{1,2,0:T(8,128)}, f32[384,768]{1,0:T(8,128)}, f32[768,1536]{1,0:T(8,128)}, f32[1536,768]{1,0:T(8,128)}) async-done(((f32[3,768,384]{1,2,0:T(8,128)}, f32[384,768]{1,0:T(8,128)}, f32[768,1536]{1,0:T(8,128)}, f32[1536,768]{1,0:T(8,128)}), (f32[3,768,384]{1,2,0:T(8,128)}, f32[384,768]{1,0:T(8,128)}, f32[768,1536]{1,0:T(8,128)}, ...) | async-done | bytes 14155792 | tf_op jit(solution)/shard_map/psum | solution.py:234
  1170.5 5.2 copy.70
  1176.8 5.5 copy.105
  (237 shorter events, 88.4 us)
Async XLA Ops:
  7.2 274.5 %copy-start = (bf16[768,1536]{1,0:T(8,128)(2,1)S(1)}, bf16[768,1536]{1,0:T(8,128)(2,1)}, u32[]{:S(2)}) copy-start(bf16[768,1536]{1,0:T(8,128)(2,1)} %param.25) | copy-start | bytes 7077892
  7.2 4.6 copy-start.37
  7.2 4.6 copy-start.39
  7.2 22.6 %all-gather.6.cloned.1.call-start = ((), (), s32[]{:S(2)}) async-start(), calls=%async_computation.4 | async-start | bytes 4718592 | tf_op jit(solution)/shard_map/all_gather | solution.py:78
  7.3 5.7 copy-start.3
  9.1 3.3 copy-start.22
  9.1 5.7 copy-start.41
  9.1 6.3 copy-start.40
  14.8 211.6 %reduce-scatter.5.cloned.1.call-start = ((), (), s32[]{:S(2)}) async-start(), calls=%async_computation.5 | async-start | bytes 4718592 | tf_op jit(solution)/shard_map/reduce_scatter | solution.py:107
  61.6 12.1 %copy-start.7 = (bf16[2048,6,64]{0,2,1:T(8,128)(2,1)S(1)}, bf16[2048,6,64]{0,2,1:T(8,128)(2,1)}, u32[]{:S(2)}) copy-start(bf16[2048,6,64]{0,2,1:T(8,128)(2,1)} %get-tuple-element.501) | copy-start | bytes 4718596 | tf_op jit(solution)/shard_map/while
  61.6 12.1 %copy-start.13 = (bf16[4,512,6,64]{1,3,2,0:T(8,128)(2,1)S(1)}, bf16[4,512,6,64]{1,3,2,0:T(8,128)(2,1)}, u32[]{:S(2)}) copy-start(bf16[4,512,6,64]{1,3,2,0:T(8,128)(2,1)} %get-tuple-element.486) | copy-start | bytes 4718596 | tf_op jit(solution)/shard_map/while
  85.4 1.1 copy-start.14
  101.4 12.1 %copy-start.7 = (bf16[2048,6,64]{0,2,1:T(8,128)(2,1)S(1)}, bf16[2048,6,64]{0,2,1:T(8,128)(2,1)}, u32[]{:S(2)}) copy-start(bf16[2048,6,64]{0,2,1:T(8,128)(2,1)} %get-tuple-element.501) | copy-start | bytes 4718596 | tf_op jit(solution)/shard_map/while
  101.4 12.1 %copy-start.13 = (bf16[4,512,6,64]{1,3,2,0:T(8,128)(2,1)S(1)}, bf16[4,512,6,64]{1,3,2,0:T(8,128)(2,1)}, u32[]{:S(2)}) copy-start(bf16[4,512,6,64]{1,3,2,0:T(8,128)(2,1)} %get-tuple-element.486) | copy-start | bytes 4718596 | tf_op jit(solution)/shard_map/while
  125.2 1.1 copy-start.14
  141.3 12.1 %copy-start.7 = (bf16[2048,6,64]{0,2,1:T(8,128)(2,1)S(1)}, bf16[2048,6,64]{0,2,1:T(8,128)(2,1)}, u32[]{:S(2)}) copy-start(bf16[2048,6,64]{0,2,1:T(8,128)(2,1)} %get-tuple-element.501) | copy-start | bytes 4718596 | tf_op jit(solution)/shard_map/while
  141.3 12.1 %copy-start.13 = (bf16[4,512,6,64]{1,3,2,0:T(8,128)(2,1)S(1)}, bf16[4,512,6,64]{1,3,2,0:T(8,128)(2,1)}, u32[]{:S(2)}) copy-start(bf16[4,512,6,64]{1,3,2,0:T(8,128)(2,1)} %get-tuple-element.486) | copy-start | bytes 4718596 | tf_op jit(solution)/shard_map/while
  165.1 1.1 copy-start.14
  181.2 12.1 %copy-start.7 = (bf16[2048,6,64]{0,2,1:T(8,128)(2,1)S(1)}, bf16[2048,6,64]{0,2,1:T(8,128)(2,1)}, u32[]{:S(2)}) copy-start(bf16[2048,6,64]{0,2,1:T(8,128)(2,1)} %get-tuple-element.501) | copy-start | bytes 4718596 | tf_op jit(solution)/shard_map/while
  181.2 12.1 %copy-start.13 = (bf16[4,512,6,64]{1,3,2,0:T(8,128)(2,1)S(1)}, bf16[4,512,6,64]{1,3,2,0:T(8,128)(2,1)}, u32[]{:S(2)}) copy-start(bf16[4,512,6,64]{1,3,2,0:T(8,128)(2,1)} %get-tuple-element.486) | copy-start | bytes 4718596 | tf_op jit(solution)/shard_map/while
  204.9 1.1 copy-start.14
  206.3 4.3 copy-start.47
  209.4 1.2 copy-start.15
  214.1 12.3 %copy-start.21 = (f32[768]{0:T(1024)S(1)}, f32[768]{0:T(1024)}, u32[]{:S(2)}) copy-start(f32[768]{0:T(1024)} %get-tuple-element.278) | copy-start | bytes 9220
  214.1 67.6 %all-gather.8.cloned.1.call-start = ((), (), s32[]{:S(2)}) async-start(), calls=%async_computation.6 | async-start | bytes 4718592 | tf_op jit(solution)/shard_map/all_gather | solution.py:115
  226.4 2.6 copy-start.4
  226.4 2.8 copy-start.8
  226.4 3.7 copy-start.26
  226.4 3.7 copy-start.36
  230.1 2.8 copy-start.42
  232.1 49.6 %copy-start.48 = (f32[1536]{0:T(1024)S(1)}, f32[1536]{0:T(1024)}, u32[]{:S(2)}) copy-start(f32[1536]{0:T(1024)} %param.26) | copy-start | bytes 18436
  232.2 63.3 %all-gather.10.cloned.1.call-start = ((), (), s32[]{:S(2)}) async-start(), calls=%async_computation.8 | async-start | bytes 4718592 | tf_op jit(solution)/shard_map/all_gather | solution.py:128
  281.6 54.1 %reduce-scatter.9.cloned.1.call-start = ((), (), s32[]{:S(2)}) async-start(), calls=%async_computation.9 | async-start | bytes 4718592 | tf_op jit(solution)/shard_map/reduce_scatter | solution.py:139
  314.9 2.6 copy-start.49
  323.9 1.7 copy-start.46
  323.9 21.7 %reduce-scatter.7.cloned.1.call-start = ((), (), s32[]{:S(2)}) async-start(), calls=%async_computation.7 | async-start | bytes 4718592 | tf_op jit(solution)/shard_map/reduce_scatter | solution.py:120
  335.2 1.4 copy-start.5
  335.2 32.4 %all-gather.12.cloned.1.call-start = ((), (), s32[]{:S(2)}) async-start(), calls=%async_computation.10 | async-start | bytes 4718592 | tf_op jit(solution)/shard_map/all_gather | solution.py:149
  336.6 3.9 copy-start.12
  340.5 5.1 copy-start.33
  351.2 1.7 copy-start.9
  354.2 499.0 %reduce-scatter.11.cloned.1.call-start = ((), (), s32[]{:S(2)}) async-start(), calls=%async_computation.11 | async-start | bytes 4718592 | tf_op jit(solution)/shard_map/reduce_scatter | solution.py:210
  376.6 4.4 copy-start.2
  720.9 5.0 copy-start.10
  741.1 429.4 %all-reduce.5.cloned.1.call-start = ((), (), s32[]{:S(2)}) async-start(), calls=%async_computation.12 | async-start | bytes 28311552 | tf_op jit(solution)/shard_map/psum | solution.py:234
  741.2 9.8 copy-start.44
  750.9 9.1 copy-start.16
  750.9 9.1 copy-start.45
  760.0 2.4 copy-start.17
  760.0 2.4 copy-start.18
  760.0 2.4 copy-start.19
  760.1 3.7 copy-start.43
  769.5 0.7 copy-start.31
  769.6 2.5 copy-start.38
  769.6 83.7 %copy-start.6 = (bf16[1024,768]{1,0:T(8,128)(2,1)S(1)}, bf16[1024,768]{1,0:T(8,128)(2,1)}, u32[]{:S(2)}) copy-start(bf16[1024,768]{1,0:T(8,128)(2,1)} %param.16) | copy-start | bytes 4718596
  769.6 83.7 %copy-start.23 = (f32[1024]{0:T(1024)S(1)}, f32[1024]{0:T(1024)}, u32[]{:S(2)}) copy-start(f32[1024]{0:T(1024)} %copy-done.22) | copy-start | bytes 12292
  769.6 83.6 %copy-start.25 = (f32[768]{0:T(1024)S(1)}, f32[768]{0:T(1024)}, u32[]{:S(2)}) copy-start(f32[768]{0:T(1024)} %copy-done.24) | copy-start | bytes 9220
  769.6 86.3 %copy-start.30 = (f32[1024]{0:T(1024)S(1)}, f32[1024]{0:T(1024)}, u32[]{:S(2)}) copy-start(f32[1024]{0:T(1024)} %copy-done.29) | copy-start | bytes 12292
  769.6 86.3 %copy-start.28 = (f32[1024]{0:T(1024)S(1)}, f32[1024]{0:T(1024)}, u32[]{:S(2)}) copy-start(f32[1024]{0:T(1024)} %copy-done.27) | copy-start | bytes 12292
  853.2 2.7 copy-start.11
  1170.5 5.3 copy-start.20
  1175.8 6.5 slice-start
  1176.8 5.5 slice-start.1
  1176.8 7.7 copy-start.1
  (6 other events, 3.9 us)
Sparse Core Ops, SparseCore 0:
  14.9 14.8 all-gather.5
  214.3 12.0 reduce-scatter.4
  232.3 13.2 all-gather.7
  281.8 7.9 all-gather.9
  324.0 6.7 reduce-scatter.8
  335.4 10.2 reduce-scatter.6
  354.3 13.2 all-gather.11
  741.2 12.0 reduce-scatter.10
  769.7 400.7 all-reduce.4
